TPU v7x, 256 devices: a whole 4x4x8 slice. The times are simulated.
256 devices in a mesh: gx: 16 (over z, core), gy: 16 (over y, x).
Axes of the slice: x: 4, y: 4, z: 8, core: 2. Of those that a mesh axis runs over, the one named last changes fastest.
Arguments:
- latent_noise: float32 [1024, 65536], P('gx', 'gy'), may hold values from -6 to 6
- kappa_sq: float32 [1024, 1024], P('gx', 'gy'), may hold values from 0.25 to 4
- obs_cell: int32 [65536], P(('gx', 'gy')), may hold values from 0 to 4095
- obs_value: float32 [65536], P(('gx', 'gy')), may hold values from -6 to 6
- obs_var: float32 [65536], P(('gx', 'gy')), may hold values from 0.1 to 1
Outputs:
- latent_new: float32 [1024, 65536], P('gx', 'gy')
- prior_field: float32 [1024, 65536], P('gx', 'gy')
Inputs may be any that keep to these rules, and one draw needn't show every extreme that they name: obs_cell[j] is a cell of the block held by device j // 256 in the order of gx+gy (gx slowest), written as row * 64 + column within that block.
All inputs are finite; a program needn't handle non-finite values.
Results may differ from a plain program's by a relative error of at most 0.0001.
Values sent between devices are 32-bit elements; how exact they have to be, the bound alone decides.
No kernel may reach another device: no remote copies, remote signals or barrier semaphores. Data moves between devices by JAX's collectives and lax.ppermute only.
A program may use at most 64 MiB of HBM per device.

v0:
```python
import jax
import jax.numpy as jnp
import numpy as np
from jax import lax
from jax.sharding import PartitionSpec as P

MEMBERS = 64
SWEEPS = 4
LOWER_EDGE = 0.25
UPPER_EDGE = 12.0


def padded(block, sides, width):
    for axis, dim in sides:
        count = lax.axis_size(axis)
        forward = [(i, i + 1) for i in range(count - 1)]
        backward = [(target, source) for source, target in forward]
        low = lax.ppermute(
            lax.slice_in_dim(block, block.shape[dim] - width, None, axis=dim), axis, forward
        )
        high = lax.ppermute(lax.slice_in_dim(block, 0, width, axis=dim), axis, backward)
        block = jnp.concatenate([low, block, high], axis=dim)
    return block


def cheb_coeffs(terms):
    angles = np.pi * (np.arange(64) + 0.5) / 64.0
    nodes = 0.5 * (UPPER_EDGE + LOWER_EDGE) + 0.5 * (UPPER_EDGE - LOWER_EDGE) * np.cos(angles)
    values = []
    for order in range(terms):
        coeff = 2.0 / 64.0 * np.sum(np.cos(order * angles) / nodes)
        if order == 0:
            coeff = 0.5 * coeff
        values.append(float(coeff))
    return values


def chol_solve(factor, rhs):
    lower_sol = lax.linalg.triangular_solve(factor, rhs, left_side=True, lower=True)
    return lax.linalg.triangular_solve(
        factor, lower_sol, left_side=True, lower=True, transpose_a=True
    )


def stencil(field, along_x, along_y, diagonal):
    beside = along_x[2:] + along_x[:-2] + along_y[:, 2 * MEMBERS :] + along_y[:, : -2 * MEMBERS]
    applied = diagonal * field - beside
    return (2.0 * applied - (UPPER_EDGE + LOWER_EDGE) * field) / (UPPER_EDGE - LOWER_EDGE)


def chebyshev(start, scaled, coeffs):
    earlier = start
    current = scaled(start)
    total = coeffs[0] * start + coeffs[1] * current
    for order in range(2, len(coeffs)):
        following = 2.0 * scaled(current) - earlier
        total = total + coeffs[order] * following
        earlier, current = (current, following)
    return total


def per_device(latent_noise, kappa_sq, obs_cell, obs_value, obs_var):
    rows_x, width = latent_noise.shape
    cells_y = width // MEMBERS
    coeffs = cheb_coeffs(SWEEPS + 1)
    diagonal = jnp.repeat(kappa_sq + 4.0, MEMBERS, axis=1)

    def scaled(field):
        along_x = padded(field, (("gx", 0),), 1)
        along_y = padded(field, (("gy", 1),), MEMBERS)
        return stencil(field, along_x, along_y, diagonal)

    prior_field = chebyshev(latent_noise, scaled, coeffs)
    field_cells = prior_field.reshape(rows_x * cells_y, MEMBERS)
    predicted = jnp.take(field_cells, obs_cell, axis=0)
    weight = 1.0 / obs_var
    misfits = obs_value[:, None] - predicted
    own_misfit = jnp.sum(misfits * misfits * weight[:, None])
    spread = predicted - jnp.mean(predicted, axis=1, keepdims=True)
    scale_down = float(MEMBERS * (MEMBERS - 1))
    misfit_total = lax.psum(own_misfit, ("gx", "gy"))
    inflation = 1.0 + misfit_total / scale_down
    scaled_spread = spread * (weight / inflation)[:, None]
    own_gram = jnp.dot(
        scaled_spread.T, spread, precision=lax.Precision.HIGHEST, preferred_element_type=jnp.float32
    )
    own_cross = jnp.dot(
        scaled_spread.T,
        misfits,
        precision=lax.Precision.HIGHEST,
        preferred_element_type=jnp.float32,
    )
    gram, cross = lax.psum((own_gram, own_cross), ("gx", "gy"))
    system = (MEMBERS - 1) * jnp.eye(MEMBERS, dtype=jnp.float32) + gram
    factor = jnp.linalg.cholesky(system)
    gain = chol_solve(factor, cross)
    latent_cells = latent_noise.reshape(rows_x * cells_y, MEMBERS)
    deviation = latent_cells - jnp.mean(latent_cells, axis=1, keepdims=True)
    update = jnp.dot(
        deviation, gain, precision=lax.Precision.HIGHEST, preferred_element_type=jnp.float32
    )
    latent_new = (latent_cells + update).reshape(rows_x, width)
    return (latent_new, prior_field)


def solution(mesh):
    placed = (P("gx", "gy"), P("gx", "gy"), P(("gx", "gy")), P(("gx", "gy")), P(("gx", "gy")))
    return jax.shard_map(
        per_device,
        mesh=mesh,
        in_specs=placed,
        out_specs=(P("gx", "gy"), P("gx", "gy")),
        check_vma=False,
    )
```

profile of v0, /device:TPU:1, one launch (start us, length us, event | category | flops | bytes accessed | tf_op | source)
XLA Modules:
  0.0 266.3 jit_solution(12779640378611144372)
XLA Ops:
  2.8 4.6 %collective-permute-start.3 = (f32[64,64]{1,0:T(8,128)S(1)}, f32[64,64]{1,0:T(8,128)S(1)}, u32[]{:S(2)}, u32[]{:S(2)}) collective-permute-start(f32[64,64]{1,0:T(8,128)S(1)} %get-tuple-element.21), channel_id=1, source_target_pairs={{0,1},{1,2},{2,3},{3,4},{4,5},{5,6},{6,7},{7,8},{8,9},{9,10},{10,1... | collective-permute-start | bytes 49160 | tf_op jit(solution)/shard_map/ppermute | solution.py:18
  8.4 5.1 %collective-permute-start = (f32[1,4096]{1,0:T(1,128)S(1)}, f32[1,4096]{1,0:T(1,128)S(1)}, u32[]{:S(2)}, u32[]{:S(2)}) collective-permute-start(f32[1,4096]{1,0:T(1,128)S(1)} %get-tuple-element.18), channel_id=1, source_target_pairs={{16,0},{32,16},{48,32},{64,48},{80,64},{96,80},{112,96},{128,112},... | collective-permute-start | bytes 49160 | tf_op jit(solution)/shard_map/ppermute | solution.py:21
  13.5 1.9 collective-permute-start.1
  15.4 2.0 reshape.43
  18.1 1.9 broadcast_in_dim.23
  20.1 3.0 %reshape.44 = f32[64,4096]{1,0:T(8,128)} reshape(f32[64,64,64]{2,1,0:T(8,128)} %broadcast_in_dim.23) | data formatting | bytes 2097152 | tf_op jit(solution)/shard_map/reshape | solution.py:66
  23.1 1.9 broadcast_multiply_fusion
  25.1 1.3 collective-permute-start.6
  26.4 4.0 %collective-permute-start.7 = (f32[64,64]{1,0:T(8,128)S(1)}, f32[64,64]{1,0:T(8,128)S(1)}, u32[]{:S(2)}, u32[]{:S(2)}) collective-permute-start(f32[64,64]{1,0:T(8,128)S(1)} %get-tuple-element.17), channel_id=1, source_target_pairs={{0,1},{1,2},{2,3},{3,4},{4,5},{5,6},{6,7},{7,8},{8,9},{9,10},{10,1... | collective-permute-start | bytes 49160 | tf_op jit(solution)/shard_map/ppermute | solution.py:18
  30.4 3.0 %collective-permute-start.4 = (f32[1,4096]{1,0:T(1,128)S(1)}, f32[1,4096]{1,0:T(1,128)S(1)}, u32[]{:S(2)}, u32[]{:S(2)}) collective-permute-start(f32[1,4096]{1,0:T(1,128)S(1)} %get-tuple-element.14), channel_id=1, source_target_pairs={{16,0},{32,16},{48,32},{64,48},{80,64},{96,80},{112,96},{128,112},... | collective-permute-start | bytes 49160 | tf_op jit(solution)/shard_map/ppermute | solution.py:21
  33.4 2.6 collective-permute-start.5
  36.9 2.0 fusion.24
  39.0 1.3 collective-permute-start.10
  40.3 4.0 %collective-permute-start.11 = (f32[64,64]{1,0:T(8,128)S(1)}, f32[64,64]{1,0:T(8,128)S(1)}, u32[]{:S(2)}, u32[]{:S(2)}) collective-permute-start(f32[64,64]{1,0:T(8,128)S(1)} %get-tuple-element.13), channel_id=1, source_target_pairs={{0,1},{1,2},{2,3},{3,4},{4,5},{5,6},{6,7},{7,8},{8,9},{9,10},{10,1... | collective-permute-start | bytes 49160 | tf_op jit(solution)/shard_map/ppermute | solution.py:18
  44.3 2.3 collective-permute-start.8
  46.5 4.4 %collective-permute-start.9 = (f32[1,4096]{1,0:T(1,128)S(1)}, f32[1,4096]{1,0:T(1,128)S(1)}, u32[]{:S(2)}, u32[]{:S(2)}) collective-permute-start(f32[1,4096]{1,0:T(1,128)S(1)} %get-tuple-element.11), channel_id=1, source_target_pairs={{0,16},{16,32},{32,48},{48,64},{64,80},{80,96},{96,112},{112,128},... | collective-permute-start | bytes 49160 | tf_op jit(solution)/shard_map/ppermute | solution.py:18
  51.8 2.0 fusion.16
  54.8 1.3 collective-permute-start.14
  56.1 4.6 %collective-permute-start.15 = (f32[64,64]{1,0:T(8,128)S(1)}, f32[64,64]{1,0:T(8,128)S(1)}, u32[]{:S(2)}, u32[]{:S(2)}) collective-permute-start(f32[64,64]{1,0:T(8,128)S(1)} %get-tuple-element.9), channel_id=1, source_target_pairs={{0,1},{1,2},{2,3},{3,4},{4,5},{5,6},{6,7},{7,8},{8,9},{9,10},{10,1... | collective-permute-start | bytes 49160 | tf_op jit(solution)/shard_map/ppermute | solution.py:18
  60.7 1.9 collective-permute-start.12
  62.6 4.5 %collective-permute-start.13 = (f32[1,4096]{1,0:T(1,128)S(1)}, f32[1,4096]{1,0:T(1,128)S(1)}, u32[]{:S(2)}, u32[]{:S(2)}) collective-permute-start(f32[1,4096]{1,0:T(1,128)S(1)} %get-tuple-element.7), channel_id=1, source_target_pairs={{0,16},{16,32},{32,48},{48,64},{64,80},{80,96},{96,112},{112,128},... | collective-permute-start | bytes 49160 | tf_op jit(solution)/shard_map/ppermute | solution.py:18
  67.2 1.6 copy.9
  68.7 5.6 %fusion.8 = f32[64,4096]{1,0:T(8,128)} fusion(f32[64,4096]{1,0:T(8,128)} %copy-done.2, f32[64,4096]{1,0:T(8,128)} %copy-done.3, f32[64,64]{1,0:T(8,128)S(1)} %collective-permute-done.15, f32[64,64]{1,0:T(8,128)S(1)} %collective-permute-done.14, f32[1,4096]{1,0:T(1,128)S(1)} %collective-permute-done.13, f32[1,4096]{1,0:T(1,128)S(1)} %collective-permute-done.12, ...), kind=kLoop, calls=%fused_computation.11 | loop fusion | flops 9175040 | bytes 5373952 | tf_op jit(solution)/shard_map/add | solution.py:57
  74.4 3.2 %reshape.45 = f32[4096,64]{1,0:T(8,128)} reshape(f32[64,4096]{1,0:T(8,128)} %fusion.8) | data formatting | bytes 2097152 | tf_op jit(solution)/shard_map/reshape | solution.py:74
  77.6 2.3 gather_fusion
  80.7 89.7 %psum.21 = f32[]{:T(128)} all-reduce(f32[]{:T(128)} %get-tuple-element.3), channel_id=1, replica_groups=mesh['gx'=16,'gy'=16] {'gx','gy'}, use_global_device_ids=true, to_apply=%region_3.4 | all-reduce | flops 1 | bytes 8 | tf_op jit(solution)/shard_map/psum | solution.py:81
  172.3 74.2 %all-reduce = (f32[64,64]{1,0:T(8,128)S(1)}, f32[64,64]{1,0:T(8,128)S(1)}) all-reduce(f32[64,64]{1,0:T(8,128)S(1)} %fusion.34, f32[64,64]{1,0:T(8,128)S(1)} %fusion.36), channel_id=1, replica_groups=mesh['gx'=16,'gy'=16] {'gx','gy'}, use_global_device_ids=true, to_apply=%region_7.8 | all-reduce | flops 8192 | bytes 65536 | tf_op jit(solution)/shard_map/psum | solution.py:93
  246.5 5.8 %cholesky.16 = f32[64,64]{1,0:T(8,128)S(1)} custom-call(f32[64,64]{1,0:T(8,128)S(1)} %fusion.57), custom_call_target="Cholesky" | custom-call | tf_op jit(solution)/shard_map/jit(cholesky)/cholesky | solution.py:95
  253.7 4.9 %custom-call.8 = f32[1,64,64]{1,2,0:T(8,128)S(1)} custom-call(f32[1,64,64]{2,1,0:T(8,128)S(1)} %fusion.52), custom_call_target="InvertDiagBlocksLowerTriangular" | custom-call | tf_op jit(solution)/shard_map/triangular_solve | solution.py:40
  259.1 3.7 %convolution_add_fusion = f32[4096,64]{0,1:T(8,128)} fusion(f32[4096,64]{0,1:T(8,128)S(1)} %copy-done.4, f32[64,64]{1,0:T(8,128)S(1)} %fusion.53, f32[4096,64]{1,0:T(8,128)S(1)} %reshape.43, f32[4096]{0:T(1024)S(1)} %broadcast_multiply_fusion.1), kind=kOutput, calls=%fused_computation.1 | convolution fusion | flops 201850880 | bytes 3178496 | tf_op jit(solution)/shard_map/dot_general | solution.py:99
  262.8 1.8 copy.10
  264.6 1.6 reshape.46
  (63 shorter events, 10.5 us)
Async XLA Ops:
  0.6 16.8 %copy-start.5 = (f32[64,64]{1,0:T(8,128)S(1)}, f32[64,64]{1,0:T(8,128)}, u32[]{:S(2)}) copy-start(f32[64,64]{1,0:T(8,128)} %param.6) | copy-start | bytes 49156
  1.5 21.5 %collective-permute-start.2 = (f32[64,64]{1,0:T(8,128)S(1)}, f32[64,64]{1,0:T(8,128)S(1)}, u32[]{:S(2)}, u32[]{:S(2)}) collective-permute-start(f32[64,64]{1,0:T(8,128)S(1)} %get-tuple-element.20), channel_id=1, source_target_pairs={{1,0},{2,1},{3,2},{4,3},{5,4},{6,5},{7,6},{8,7},{9,8},{10,9},{11,1... | collective-permute-start | bytes 49160 | tf_op jit(solution)/shard_map/ppermute | solution.py:21
  2.8 20.3 %collective-permute-start.3 = (f32[64,64]{1,0:T(8,128)S(1)}, f32[64,64]{1,0:T(8,128)S(1)}, u32[]{:S(2)}, u32[]{:S(2)}) collective-permute-start(f32[64,64]{1,0:T(8,128)S(1)} %get-tuple-element.21), channel_id=1, source_target_pairs={{0,1},{1,2},{2,3},{3,4},{4,5},{5,6},{6,7},{7,8},{8,9},{9,10},{10,1... | collective-permute-start | bytes 49160 | tf_op jit(solution)/shard_map/ppermute | solution.py:18
  8.4 14.7 %collective-permute-start = (f32[1,4096]{1,0:T(1,128)S(1)}, f32[1,4096]{1,0:T(1,128)S(1)}, u32[]{:S(2)}, u32[]{:S(2)}) collective-permute-start(f32[1,4096]{1,0:T(1,128)S(1)} %get-tuple-element.18), channel_id=1, source_target_pairs={{16,0},{32,16},{48,32},{64,48},{80,64},{96,80},{112,96},{128,112},... | collective-permute-start | bytes 49160 | tf_op jit(solution)/shard_map/ppermute | solution.py:21
  13.5 4.6 %copy-start.8 = (s32[256]{0:T(256)S(1)}, s32[256]{0:T(256)}, u32[]{:S(2)}) copy-start(s32[256]{0:T(256)} %param.7) | copy-start | bytes 3076
  13.5 9.6 %collective-permute-start.1 = (f32[1,4096]{1,0:T(1,128)S(1)}, f32[1,4096]{1,0:T(1,128)S(1)}, u32[]{:S(2)}, u32[]{:S(2)}) collective-permute-start(f32[1,4096]{1,0:T(1,128)S(1)} %get-tuple-element.19), channel_id=1, source_target_pairs={{0,16},{16,32},{32,48},{48,64},{64,80},{80,96},{96,112},{112,128},... | collective-permute-start | bytes 49160 | tf_op jit(solution)/shard_map/ppermute | solution.py:18
  20.1 3.0 %copy-start = (f32[64,4096]{1,0:T(8,128)S(1)}, f32[64,4096]{1,0:T(8,128)}, u32[]{:S(2)}) copy-start(f32[64,4096]{1,0:T(8,128)} %param.5) | copy-start | bytes 3145732
  23.0 13.0 %copy-start.6 = (f32[256]{0:T(256)S(1)}, f32[256]{0:T(256)}, u32[]{:S(2)}) copy-start(f32[256]{0:T(256)} %param.9) | copy-start | bytes 3076
  23.0 13.8 %copy-start.1 = (f32[64,4096]{1,0:T(8,128)S(1)}, f32[64,4096]{1,0:T(8,128)}, u32[]{:S(2)}) copy-start(f32[64,4096]{1,0:T(8,128)} %reshape.44) | copy-start | bytes 3145732
  25.1 10.9 %collective-permute-start.6 = (f32[64,64]{1,0:T(8,128)S(1)}, f32[64,64]{1,0:T(8,128)S(1)}, u32[]{:S(2)}, u32[]{:S(2)}) collective-permute-start(f32[64,64]{1,0:T(8,128)S(1)} %get-tuple-element.16), channel_id=1, source_target_pairs={{1,0},{2,1},{3,2},{4,3},{5,4},{6,5},{7,6},{8,7},{9,8},{10,9},{11,1... | collective-permute-start | bytes 49160 | tf_op jit(solution)/shard_map/ppermute | solution.py:21
  26.4 9.6 %collective-permute-start.7 = (f32[64,64]{1,0:T(8,128)S(1)}, f32[64,64]{1,0:T(8,128)S(1)}, u32[]{:S(2)}, u32[]{:S(2)}) collective-permute-start(f32[64,64]{1,0:T(8,128)S(1)} %get-tuple-element.17), channel_id=1, source_target_pairs={{0,1},{1,2},{2,3},{3,4},{4,5},{5,6},{6,7},{7,8},{8,9},{9,10},{10,1... | collective-permute-start | bytes 49160 | tf_op jit(solution)/shard_map/ppermute | solution.py:18
  30.4 5.6 %collective-permute-start.4 = (f32[1,4096]{1,0:T(1,128)S(1)}, f32[1,4096]{1,0:T(1,128)S(1)}, u32[]{:S(2)}, u32[]{:S(2)}) collective-permute-start(f32[1,4096]{1,0:T(1,128)S(1)} %get-tuple-element.14), channel_id=1, source_target_pairs={{16,0},{32,16},{48,32},{64,48},{80,64},{96,80},{112,96},{128,112},... | collective-permute-start | bytes 49160 | tf_op jit(solution)/shard_map/ppermute | solution.py:21
  33.4 3.5 %collective-permute-start.5 = (f32[1,4096]{1,0:T(1,128)S(1)}, f32[1,4096]{1,0:T(1,128)S(1)}, u32[]{:S(2)}, u32[]{:S(2)}) collective-permute-start(f32[1,4096]{1,0:T(1,128)S(1)} %get-tuple-element.15), channel_id=1, source_target_pairs={{0,16},{16,32},{32,48},{48,64},{64,80},{80,96},{96,112},{112,128},... | collective-permute-start | bytes 49160 | tf_op jit(solution)/shard_map/ppermute | solution.py:18
  38.8 15.0 %copy-start.2 = (f32[64,4096]{1,0:T(8,128)}, f32[64,4096]{1,0:T(8,128)S(1)}, u32[]{:S(2)}) copy-start(f32[64,4096]{1,0:T(8,128)S(1)} %fusion.24) | copy-start | bytes 3145732
  39.0 12.0 %collective-permute-start.10 = (f32[64,64]{1,0:T(8,128)S(1)}, f32[64,64]{1,0:T(8,128)S(1)}, u32[]{:S(2)}, u32[]{:S(2)}) collective-permute-start(f32[64,64]{1,0:T(8,128)S(1)} %get-tuple-element.12), channel_id=1, source_target_pairs={{1,0},{2,1},{3,2},{4,3},{5,4},{6,5},{7,6},{8,7},{9,8},{10,9},{11,1... | collective-permute-start | bytes 49160 | tf_op jit(solution)/shard_map/ppermute | solution.py:21
  40.3 10.7 %collective-permute-start.11 = (f32[64,64]{1,0:T(8,128)S(1)}, f32[64,64]{1,0:T(8,128)S(1)}, u32[]{:S(2)}, u32[]{:S(2)}) collective-permute-start(f32[64,64]{1,0:T(8,128)S(1)} %get-tuple-element.13), channel_id=1, source_target_pairs={{0,1},{1,2},{2,3},{3,4},{4,5},{5,6},{6,7},{7,8},{8,9},{9,10},{10,1... | collective-permute-start | bytes 49160 | tf_op jit(solution)/shard_map/ppermute | solution.py:18
  44.3 6.7 %collective-permute-start.8 = (f32[1,4096]{1,0:T(1,128)S(1)}, f32[1,4096]{1,0:T(1,128)S(1)}, u32[]{:S(2)}, u32[]{:S(2)}) collective-permute-start(f32[1,4096]{1,0:T(1,128)S(1)} %get-tuple-element.10), channel_id=1, source_target_pairs={{16,0},{32,16},{48,32},{64,48},{80,64},{96,80},{112,96},{128,112},... | collective-permute-start | bytes 49160 | tf_op jit(solution)/shard_map/ppermute | solution.py:21
  46.5 5.3 %collective-permute-start.9 = (f32[1,4096]{1,0:T(1,128)S(1)}, f32[1,4096]{1,0:T(1,128)S(1)}, u32[]{:S(2)}, u32[]{:S(2)}) collective-permute-start(f32[1,4096]{1,0:T(1,128)S(1)} %get-tuple-element.11), channel_id=1, source_target_pairs={{0,16},{16,32},{32,48},{48,64},{64,80},{80,96},{96,112},{112,128},... | collective-permute-start | bytes 49160 | tf_op jit(solution)/shard_map/ppermute | solution.py:18
  53.8 1.0 copy-start.3
  54.8 13.9 %collective-permute-start.14 = (f32[64,64]{1,0:T(8,128)S(1)}, f32[64,64]{1,0:T(8,128)S(1)}, u32[]{:S(2)}, u32[]{:S(2)}) collective-permute-start(f32[64,64]{1,0:T(8,128)S(1)} %get-tuple-element.8), channel_id=1, source_target_pairs={{1,0},{2,1},{3,2},{4,3},{5,4},{6,5},{7,6},{8,7},{9,8},{10,9},{11,1... | collective-permute-start | bytes 49160 | tf_op jit(solution)/shard_map/ppermute | solution.py:21
  56.1 12.6 %collective-permute-start.15 = (f32[64,64]{1,0:T(8,128)S(1)}, f32[64,64]{1,0:T(8,128)S(1)}, u32[]{:S(2)}, u32[]{:S(2)}) collective-permute-start(f32[64,64]{1,0:T(8,128)S(1)} %get-tuple-element.9), channel_id=1, source_target_pairs={{0,1},{1,2},{2,3},{3,4},{4,5},{5,6},{6,7},{7,8},{8,9},{9,10},{10,1... | collective-permute-start | bytes 49160 | tf_op jit(solution)/shard_map/ppermute | solution.py:18
  60.7 8.0 %collective-permute-start.12 = (f32[1,4096]{1,0:T(1,128)S(1)}, f32[1,4096]{1,0:T(1,128)S(1)}, u32[]{:S(2)}, u32[]{:S(2)}) collective-permute-start(f32[1,4096]{1,0:T(1,128)S(1)} %get-tuple-element.6), channel_id=1, source_target_pairs={{16,0},{32,16},{48,32},{64,48},{80,64},{96,80},{112,96},{128,112},... | collective-permute-start | bytes 49160 | tf_op jit(solution)/shard_map/ppermute | solution.py:21
  62.6 6.1 %collective-permute-start.13 = (f32[1,4096]{1,0:T(1,128)S(1)}, f32[1,4096]{1,0:T(1,128)S(1)}, u32[]{:S(2)}, u32[]{:S(2)}) collective-permute-start(f32[1,4096]{1,0:T(1,128)S(1)} %get-tuple-element.7), channel_id=1, source_target_pairs={{0,16},{16,32},{32,48},{48,64},{64,80},{80,96},{96,112},{112,128},... | collective-permute-start | bytes 49160 | tf_op jit(solution)/shard_map/ppermute | solution.py:18
  74.4 5.5 %copy-start.7 = (f32[256]{0:T(256)S(1)}, f32[256]{0:T(256)}, u32[]{:S(2)}) copy-start(f32[256]{0:T(256)} %param.8) | copy-start | bytes 3076
  74.4 184.7 %copy-start.4 = (f32[4096,64]{0,1:T(8,128)S(1)}, f32[4096,64]{0,1:T(8,128)}, u32[]{:S(2)}) copy-start(f32[4096,64]{0,1:T(8,128)} %copy.9) | copy-start | bytes 3145732
where the time goes:
time: 267 us; the launch traced here: 266 us
  blocking collectives  164 us (61%)
  starting transfers between devices  48 us (18%)
  other arithmetic  25.1 us (9%)
  local copies, waits for them, and re-layouts  20.6 us (8%)
  matrix products  5.31 us (2%)
    psum x1, blocking collectives, per_device(): misfit_total = lax.psum(own_misfit, ('gx', 'gy'))  89.7 us
    psum x1, blocking collectives, per_device(): gram, cross = lax.psum((own_gram, own_cross), ('gx', 'gy'))  74.2 us
    ppermute x8, starting transfers between devices, padded(): lax.ppermute(lax.slice_in_dim(block, block.shape[dim] - width, None, axis...  30.6 us
    ppermute x8, starting transfers between devices, padded(): lax.ppermute(lax.slice_in_dim(block, 0, width, axis=dim), axis, backward)  17.4 us
    another operation x3, other arithmetic, per_device(): factor = jnp.linalg.cholesky(system)  6.55 us
    add x1, other arithmetic, chebyshev(): total = total + coeffs[order] * following  5.64 us
    another operation x2, other arithmetic, chol_solve(): lax.linalg.triangular_solve(factor, lower_sol, left_side=True, lower=True...  5.53 us
  transfers between devices with their start and end apart: 16, of which 2 were waited for; matrix products, arithmetic and copies ran while one was open for 4% of the time, Pallas kernels for 0%

commit v1 on v0

--- a/solution.py
+++ b/solution.py
@@ -90,7 +90,8 @@
         precision=lax.Precision.HIGHEST,
         preferred_element_type=jnp.float32,
     )
-    gram, cross = lax.psum((own_gram, own_cross), ("gx", "gy"))
+    cut_links = lambda piece_in: lax.psum(lax.psum(piece_in, axis_name="gy"), "gx")
+    gram, cross = cut_links((own_gram, own_cross))
     system = (MEMBERS - 1) * jnp.eye(MEMBERS, dtype=jnp.float32) + gram
     factor = jnp.linalg.cholesky(system)
     gain = chol_solve(factor, cross)

time: 267 us -> 307 us (1.15)
  blocking collectives: 164 us -> 204 us
    psum x1 -> x2, blocking collectives: 74.2 us -> 114 us  [the longest x1 57 us: per_device(): lax.psum(lax.psum(piece_in, axis_name='gy'), 'gx')]
  transfers between devices with their start and end apart: 16 -> 16, of which waited for: 2 -> 2; matrix products, arithmetic and copies ran while one was open for 4% -> 3% of each run, Pallas kernels for 0% -> 0%
where the time goes in v1:
time: 307 us; the launch traced here: 306 us
  blocking collectives  204 us (66%)
  starting transfers between devices  48 us (16%)
  other arithmetic  25 us (8%)
  local copies, waits for them, and re-layouts  20.6 us (7%)
  matrix products  5.31 us (2%)
    psum x1, blocking collectives, per_device(): misfit_total = lax.psum(own_misfit, ('gx', 'gy'))  89.7 us
    psum x1, blocking collectives, per_device(): lax.psum(lax.psum(piece_in, axis_name='gy'), 'gx')  57 us
    psum x1, blocking collectives, per_device(): lax.psum(piece_in, axis_name='gy')  57 us
    ppermute x8, starting transfers between devices, padded(): lax.ppermute(lax.slice_in_dim(block, block.shape[dim] - width, None, axis...  30.6 us
    ppermute x8, starting transfers between devices, padded(): lax.ppermute(lax.slice_in_dim(block, 0, width, axis=dim), axis, backward)  17.4 us
    another operation x3, other arithmetic, per_device(): factor = jnp.linalg.cholesky(system)  6.54 us
  transfers between devices with their start and end apart: 16, of which 2 were waited for; matrix products, arithmetic and copies ran while one was open for 3% of the time, Pallas kernels for 0%

profile of v1, /device:TPU:1, one launch (start us, length us, event | category | flops | bytes accessed | tf_op | source)
XLA Modules:
  0.0 305.9 jit_solution(369535335735685167)
XLA Ops:
  2.8 4.6 %collective-permute-start.3 = (f32[64,64]{1,0:T(8,128)S(1)}, f32[64,64]{1,0:T(8,128)S(1)}, u32[]{:S(2)}, u32[]{:S(2)}) collective-permute-start(f32[64,64]{1,0:T(8,128)S(1)} %get-tuple-element.23), channel_id=1, source_target_pairs={{0,1},{1,2},{2,3},{3,4},{4,5},{5,6},{6,7},{7,8},{8,9},{9,10},{10,1... | collective-permute-start | bytes 49160 | tf_op jit(solution)/shard_map/ppermute | solution.py:18
  8.4 5.1 %collective-permute-start = (f32[1,4096]{1,0:T(1,128)S(1)}, f32[1,4096]{1,0:T(1,128)S(1)}, u32[]{:S(2)}, u32[]{:S(2)}) collective-permute-start(f32[1,4096]{1,0:T(1,128)S(1)} %get-tuple-element.20), channel_id=1, source_target_pairs={{16,0},{32,16},{48,32},{64,48},{80,64},{96,80},{112,96},{128,112},... | collective-permute-start | bytes 49160 | tf_op jit(solution)/shard_map/ppermute | solution.py:21
  13.5 1.9 collective-permute-start.1
  15.4 2.0 reshape.43
  18.1 1.9 broadcast_in_dim.23
  20.1 3.0 reshape.44
  23.1 1.9 broadcast_multiply_fusion
  26.4 4.0 %collective-permute-start.7 = (f32[64,64]{1,0:T(8,128)S(1)}, f32[64,64]{1,0:T(8,128)S(1)}, u32[]{:S(2)}, u32[]{:S(2)}) collective-permute-start(f32[64,64]{1,0:T(8,128)S(1)} %get-tuple-element.19), channel_id=1, source_target_pairs={{0,1},{1,2},{2,3},{3,4},{4,5},{5,6},{6,7},{7,8},{8,9},{9,10},{10,1... | collective-permute-start | bytes 49160 | tf_op jit(solution)/shard_map/ppermute | solution.py:18
  30.4 3.0 collective-permute-start.4
  33.4 2.6 collective-permute-start.5
  36.8 2.0 fusion.24
  38.9 1.3 collective-permute-start.10
  40.2 4.0 %collective-permute-start.11 = (f32[64,64]{1,0:T(8,128)S(1)}, f32[64,64]{1,0:T(8,128)S(1)}, u32[]{:S(2)}, u32[]{:S(2)}) collective-permute-start(f32[64,64]{1,0:T(8,128)S(1)} %get-tuple-element.15), channel_id=1, source_target_pairs={{0,1},{1,2},{2,3},{3,4},{4,5},{5,6},{6,7},{7,8},{8,9},{9,10},{10,1... | collective-permute-start | bytes 49160 | tf_op jit(solution)/shard_map/ppermute | solution.py:18
  44.2 2.3 collective-permute-start.8
  46.5 4.4 %collective-permute-start.9 = (f32[1,4096]{1,0:T(1,128)S(1)}, f32[1,4096]{1,0:T(1,128)S(1)}, u32[]{:S(2)}, u32[]{:S(2)}) collective-permute-start(f32[1,4096]{1,0:T(1,128)S(1)} %get-tuple-element.13), channel_id=1, source_target_pairs={{0,16},{16,32},{32,48},{48,64},{64,80},{80,96},{96,112},{112,128},... | collective-permute-start | bytes 49160 | tf_op jit(solution)/shard_map/ppermute | solution.py:18
  51.8 2.0 fusion.16
  54.8 1.3 collective-permute-start.14
  56.1 4.6 %collective-permute-start.15 = (f32[64,64]{1,0:T(8,128)S(1)}, f32[64,64]{1,0:T(8,128)S(1)}, u32[]{:S(2)}, u32[]{:S(2)}) collective-permute-start(f32[64,64]{1,0:T(8,128)S(1)} %get-tuple-element.11), channel_id=1, source_target_pairs={{0,1},{1,2},{2,3},{3,4},{4,5},{5,6},{6,7},{7,8},{8,9},{9,10},{10,1... | collective-permute-start | bytes 49160 | tf_op jit(solution)/shard_map/ppermute | solution.py:18
  60.7 1.9 collective-permute-start.12
  62.6 4.5 %collective-permute-start.13 = (f32[1,4096]{1,0:T(1,128)S(1)}, f32[1,4096]{1,0:T(1,128)S(1)}, u32[]{:S(2)}, u32[]{:S(2)}) collective-permute-start(f32[1,4096]{1,0:T(1,128)S(1)} %get-tuple-element.9), channel_id=1, source_target_pairs={{0,16},{16,32},{32,48},{48,64},{64,80},{80,96},{96,112},{112,128},... | collective-permute-start | bytes 49160 | tf_op jit(solution)/shard_map/ppermute | solution.py:18
  67.2 1.6 copy.9
  68.7 5.5 %fusion.8 = f32[64,4096]{1,0:T(8,128)} fusion(f32[64,4096]{1,0:T(8,128)} %copy-done.2, f32[64,4096]{1,0:T(8,128)} %copy-done.3, f32[64,64]{1,0:T(8,128)S(1)} %collective-permute-done.15, f32[64,64]{1,0:T(8,128)S(1)} %collective-permute-done.14, f32[1,4096]{1,0:T(1,128)S(1)} %collective-permute-done.13, f32[1,4096]{1,0:T(1,128)S(1)} %collective-permute-done.12, ...), kind=kLoop, calls=%fused_computation.11 | loop fusion | flops 9175040 | bytes 5373952 | tf_op jit(solution)/shard_map/add | solution.py:57
  74.3 3.2 %reshape.45 = f32[4096,64]{1,0:T(8,128)} reshape(f32[64,4096]{1,0:T(8,128)} %fusion.8) | data formatting | bytes 2097152 | tf_op jit(solution)/shard_map/reshape | solution.py:74
  77.5 2.3 gather_fusion
  80.6 89.7 %psum.35 = f32[]{:T(128)} all-reduce(f32[]{:T(128)} %get-tuple-element.3), channel_id=1, replica_groups=mesh['gx'=16,'gy'=16] {'gx','gy'}, use_global_device_ids=true, to_apply=%region_3.4 | all-reduce | flops 1 | bytes 8 | tf_op jit(solution)/shard_map/psum | solution.py:81
  172.1 57.0 %all-reduce = (f32[64,64]{1,0:T(8,128)S(1)}, f32[64,64]{1,0:T(8,128)S(1)}) all-reduce(f32[64,64]{1,0:T(8,128)S(1)} %fusion.34, f32[64,64]{1,0:T(8,128)S(1)} %fusion.36), channel_id=1, replica_groups=mesh['gx'=16,'gy'=16] {'gy'}, use_global_device_ids=true, to_apply=%region_8.9 | all-reduce | flops 8192 | bytes 65536 | tf_op jit(solution)/shard_map/psum | solution.py:93
  229.1 57.0 %all-reduce.1 = (f32[64,64]{1,0:T(8,128)S(1)}, f32[64,64]{1,0:T(8,128)S(1)}) all-reduce(f32[64,64]{1,0:T(8,128)S(1)} %get-tuple-element.4, f32[64,64]{1,0:T(8,128)S(1)} %get-tuple-element.5), channel_id=1, replica_groups=mesh['gx'=16,'gy'=16] {'gx'}, use_global_device_ids=true, to_apply=%region_9.10 | all-reduce | flops 8192 | bytes 65536 | tf_op jit(solution)/shard_map/psum | solution.py:93
  286.2 5.8 %cholesky.16 = f32[64,64]{1,0:T(8,128)S(1)} custom-call(f32[64,64]{1,0:T(8,128)S(1)} %fusion.57), custom_call_target="Cholesky" | custom-call | tf_op jit(solution)/shard_map/jit(cholesky)/cholesky | solution.py:96
  293.4 4.9 %custom-call.8 = f32[1,64,64]{1,2,0:T(8,128)S(1)} custom-call(f32[1,64,64]{2,1,0:T(8,128)S(1)} %fusion.52), custom_call_target="InvertDiagBlocksLowerTriangular" | custom-call | tf_op jit(solution)/shard_map/triangular_solve | solution.py:40
  298.8 3.7 %convolution_add_fusion = f32[4096,64]{0,1:T(8,128)} fusion(f32[4096,64]{0,1:T(8,128)S(1)} %copy-done.4, f32[64,64]{1,0:T(8,128)S(1)} %fusion.53, f32[4096,64]{1,0:T(8,128)S(1)} %reshape.43, f32[4096]{0:T(1024)S(1)} %broadcast_multiply_fusion.1), kind=kOutput, calls=%fused_computation.1 | convolution fusion | flops 201850880 | bytes 3178496 | tf_op jit(solution)/shard_map/dot_general | solution.py:100
  302.5 1.8 copy.10
  304.3 1.6 reshape.46
  (64 shorter events, 11.8 us)
Async XLA Ops:
  0.6 16.8 %copy-start.5 = (f32[64,64]{1,0:T(8,128)S(1)}, f32[64,64]{1,0:T(8,128)}, u32[]{:S(2)}) copy-start(f32[64,64]{1,0:T(8,128)} %param.6) | copy-start | bytes 49156
  1.5 21.5 %collective-permute-start.2 = (f32[64,64]{1,0:T(8,128)S(1)}, f32[64,64]{1,0:T(8,128)S(1)}, u32[]{:S(2)}, u32[]{:S(2)}) collective-permute-start(f32[64,64]{1,0:T(8,128)S(1)} %get-tuple-element.22), channel_id=1, source_target_pairs={{1,0},{2,1},{3,2},{4,3},{5,4},{6,5},{7,6},{8,7},{9,8},{10,9},{11,1... | collective-permute-start | bytes 49160 | tf_op jit(solution)/shard_map/ppermute | solution.py:21
  2.8 20.3 %collective-permute-start.3 = (f32[64,64]{1,0:T(8,128)S(1)}, f32[64,64]{1,0:T(8,128)S(1)}, u32[]{:S(2)}, u32[]{:S(2)}) collective-permute-start(f32[64,64]{1,0:T(8,128)S(1)} %get-tuple-element.23), channel_id=1, source_target_pairs={{0,1},{1,2},{2,3},{3,4},{4,5},{5,6},{6,7},{7,8},{8,9},{9,10},{10,1... | collective-permute-start | bytes 49160 | tf_op jit(solution)/shard_map/ppermute | solution.py:18
  8.4 14.7 %collective-permute-start = (f32[1,4096]{1,0:T(1,128)S(1)}, f32[1,4096]{1,0:T(1,128)S(1)}, u32[]{:S(2)}, u32[]{:S(2)}) collective-permute-start(f32[1,4096]{1,0:T(1,128)S(1)} %get-tuple-element.20), channel_id=1, source_target_pairs={{16,0},{32,16},{48,32},{64,48},{80,64},{96,80},{112,96},{128,112},... | collective-permute-start | bytes 49160 | tf_op jit(solution)/shard_map/ppermute | solution.py:21
  13.5 4.6 %copy-start.8 = (s32[256]{0:T(256)S(1)}, s32[256]{0:T(256)}, u32[]{:S(2)}) copy-start(s32[256]{0:T(256)} %param.7) | copy-start | bytes 3076
  13.5 9.6 %collective-permute-start.1 = (f32[1,4096]{1,0:T(1,128)S(1)}, f32[1,4096]{1,0:T(1,128)S(1)}, u32[]{:S(2)}, u32[]{:S(2)}) collective-permute-start(f32[1,4096]{1,0:T(1,128)S(1)} %get-tuple-element.21), channel_id=1, source_target_pairs={{0,16},{16,32},{32,48},{48,64},{64,80},{80,96},{96,112},{112,128},... | collective-permute-start | bytes 49160 | tf_op jit(solution)/shard_map/ppermute | solution.py:18
  20.1 3.0 copy-start
  23.0 13.0 %copy-start.6 = (f32[256]{0:T(256)S(1)}, f32[256]{0:T(256)}, u32[]{:S(2)}) copy-start(f32[256]{0:T(256)} %param.9) | copy-start | bytes 3076
  23.0 13.8 %copy-start.1 = (f32[64,4096]{1,0:T(8,128)S(1)}, f32[64,4096]{1,0:T(8,128)}, u32[]{:S(2)}) copy-start(f32[64,4096]{1,0:T(8,128)} %reshape.44) | copy-start | bytes 3145732
  25.1 10.9 %collective-permute-start.6 = (f32[64,64]{1,0:T(8,128)S(1)}, f32[64,64]{1,0:T(8,128)S(1)}, u32[]{:S(2)}, u32[]{:S(2)}) collective-permute-start(f32[64,64]{1,0:T(8,128)S(1)} %get-tuple-element.18), channel_id=1, source_target_pairs={{1,0},{2,1},{3,2},{4,3},{5,4},{6,5},{7,6},{8,7},{9,8},{10,9},{11,1... | collective-permute-start | bytes 49160 | tf_op jit(solution)/shard_map/ppermute | solution.py:21
  26.4 9.6 %collective-permute-start.7 = (f32[64,64]{1,0:T(8,128)S(1)}, f32[64,64]{1,0:T(8,128)S(1)}, u32[]{:S(2)}, u32[]{:S(2)}) collective-permute-start(f32[64,64]{1,0:T(8,128)S(1)} %get-tuple-element.19), channel_id=1, source_target_pairs={{0,1},{1,2},{2,3},{3,4},{4,5},{5,6},{6,7},{7,8},{8,9},{9,10},{10,1... | collective-permute-start | bytes 49160 | tf_op jit(solution)/shard_map/ppermute | solution.py:18
  30.4 5.6 %collective-permute-start.4 = (f32[1,4096]{1,0:T(1,128)S(1)}, f32[1,4096]{1,0:T(1,128)S(1)}, u32[]{:S(2)}, u32[]{:S(2)}) collective-permute-start(f32[1,4096]{1,0:T(1,128)S(1)} %get-tuple-element.16), channel_id=1, source_target_pairs={{16,0},{32,16},{48,32},{64,48},{80,64},{96,80},{112,96},{128,112},... | collective-permute-start | bytes 49160 | tf_op jit(solution)/shard_map/ppermute | solution.py:21
  33.4 3.5 %collective-permute-start.5 = (f32[1,4096]{1,0:T(1,128)S(1)}, f32[1,4096]{1,0:T(1,128)S(1)}, u32[]{:S(2)}, u32[]{:S(2)}) collective-permute-start(f32[1,4096]{1,0:T(1,128)S(1)} %get-tuple-element.17), channel_id=1, source_target_pairs={{0,16},{16,32},{32,48},{48,64},{64,80},{80,96},{96,112},{112,128},... | collective-permute-start | bytes 49160 | tf_op jit(solution)/shard_map/ppermute | solution.py:18
  38.8 15.0 %copy-start.2 = (f32[64,4096]{1,0:T(8,128)}, f32[64,4096]{1,0:T(8,128)S(1)}, u32[]{:S(2)}) copy-start(f32[64,4096]{1,0:T(8,128)S(1)} %fusion.24) | copy-start | bytes 3145732
  38.9 12.0 %collective-permute-start.10 = (f32[64,64]{1,0:T(8,128)S(1)}, f32[64,64]{1,0:T(8,128)S(1)}, u32[]{:S(2)}, u32[]{:S(2)}) collective-permute-start(f32[64,64]{1,0:T(8,128)S(1)} %get-tuple-element.14), channel_id=1, source_target_pairs={{1,0},{2,1},{3,2},{4,3},{5,4},{6,5},{7,6},{8,7},{9,8},{10,9},{11,1... | collective-permute-start | bytes 49160 | tf_op jit(solution)/shard_map/ppermute | solution.py:21
  40.2 10.7 %collective-permute-start.11 = (f32[64,64]{1,0:T(8,128)S(1)}, f32[64,64]{1,0:T(8,128)S(1)}, u32[]{:S(2)}, u32[]{:S(2)}) collective-permute-start(f32[64,64]{1,0:T(8,128)S(1)} %get-tuple-element.15), channel_id=1, source_target_pairs={{0,1},{1,2},{2,3},{3,4},{4,5},{5,6},{6,7},{7,8},{8,9},{9,10},{10,1... | collective-permute-start | bytes 49160 | tf_op jit(solution)/shard_map/ppermute | solution.py:18
  44.2 6.7 %collective-permute-start.8 = (f32[1,4096]{1,0:T(1,128)S(1)}, f32[1,4096]{1,0:T(1,128)S(1)}, u32[]{:S(2)}, u32[]{:S(2)}) collective-permute-start(f32[1,4096]{1,0:T(1,128)S(1)} %get-tuple-element.12), channel_id=1, source_target_pairs={{16,0},{32,16},{48,32},{64,48},{80,64},{96,80},{112,96},{128,112},... | collective-permute-start | bytes 49160 | tf_op jit(solution)/shard_map/ppermute | solution.py:21
  46.5 5.3 %collective-permute-start.9 = (f32[1,4096]{1,0:T(1,128)S(1)}, f32[1,4096]{1,0:T(1,128)S(1)}, u32[]{:S(2)}, u32[]{:S(2)}) collective-permute-start(f32[1,4096]{1,0:T(1,128)S(1)} %get-tuple-element.13), channel_id=1, source_target_pairs={{0,16},{16,32},{32,48},{48,64},{64,80},{80,96},{96,112},{112,128},... | collective-permute-start | bytes 49160 | tf_op jit(solution)/shard_map/ppermute | solution.py:18
  53.8 1.0 copy-start.3
  54.8 13.9 %collective-permute-start.14 = (f32[64,64]{1,0:T(8,128)S(1)}, f32[64,64]{1,0:T(8,128)S(1)}, u32[]{:S(2)}, u32[]{:S(2)}) collective-permute-start(f32[64,64]{1,0:T(8,128)S(1)} %get-tuple-element.10), channel_id=1, source_target_pairs={{1,0},{2,1},{3,2},{4,3},{5,4},{6,5},{7,6},{8,7},{9,8},{10,9},{11,1... | collective-permute-start | bytes 49160 | tf_op jit(solution)/shard_map/ppermute | solution.py:21
  56.1 12.6 %collective-permute-start.15 = (f32[64,64]{1,0:T(8,128)S(1)}, f32[64,64]{1,0:T(8,128)S(1)}, u32[]{:S(2)}, u32[]{:S(2)}) collective-permute-start(f32[64,64]{1,0:T(8,128)S(1)} %get-tuple-element.11), channel_id=1, source_target_pairs={{0,1},{1,2},{2,3},{3,4},{4,5},{5,6},{6,7},{7,8},{8,9},{9,10},{10,1... | collective-permute-start | bytes 49160 | tf_op jit(solution)/shard_map/ppermute | solution.py:18
  60.7 8.0 %collective-permute-start.12 = (f32[1,4096]{1,0:T(1,128)S(1)}, f32[1,4096]{1,0:T(1,128)S(1)}, u32[]{:S(2)}, u32[]{:S(2)}) collective-permute-start(f32[1,4096]{1,0:T(1,128)S(1)} %get-tuple-element.8), channel_id=1, source_target_pairs={{16,0},{32,16},{48,32},{64,48},{80,64},{96,80},{112,96},{128,112},... | collective-permute-start | bytes 49160 | tf_op jit(solution)/shard_map/ppermute | solution.py:21
  62.6 6.1 %collective-permute-start.13 = (f32[1,4096]{1,0:T(1,128)S(1)}, f32[1,4096]{1,0:T(1,128)S(1)}, u32[]{:S(2)}, u32[]{:S(2)}) collective-permute-start(f32[1,4096]{1,0:T(1,128)S(1)} %get-tuple-element.9), channel_id=1, source_target_pairs={{0,16},{16,32},{32,48},{48,64},{64,80},{80,96},{96,112},{112,128},... | collective-permute-start | bytes 49160 | tf_op jit(solution)/shard_map/ppermute | solution.py:18
  74.3 5.5 %copy-start.7 = (f32[256]{0:T(256)S(1)}, f32[256]{0:T(256)}, u32[]{:S(2)}) copy-start(f32[256]{0:T(256)} %param.8) | copy-start | bytes 3076
  74.3 224.5 %copy-start.4 = (f32[4096,64]{0,1:T(8,128)S(1)}, f32[4096,64]{0,1:T(8,128)}, u32[]{:S(2)}) copy-start(f32[4096,64]{0,1:T(8,128)} %copy.9) | copy-start | bytes 3145732
